TPU v7x, 128 devices: a whole 4x4x4 slice. The times are simulated.
128 devices in a mesh: rep: 32 (over z, y, core), tensor: 4 (over x).
Axes of the slice: x: 4, y: 4, z: 4, core: 2. Of those that a mesh axis runs over, the one named last changes fastest.
Arguments:
- hidden_in: bfloat16 [2048, 4096], P('rep', 'tensor'), may hold values from -25 to 25
- query: bfloat16 [2048, 4096], P('rep', 'tensor'), may hold values from -6 to 6
- new_kv: bfloat16 [2048, 2, 512], P('rep', None, 'tensor'), may hold values from -8 to 8
- pool: bfloat16 [4096, 128, 2, 512], P('rep', None, None, 'tensor'), may hold values from -8 to 8
- page_table: int32 [2048, 2], P('rep'), may hold values from 0 to 127, as said below
- lengths: int32 [2048], replicated, may hold values from 1 to 256, 262144 in all
- dest: int32 [32], replicated, may hold values from 0 to 31, each once
- out_weight: bfloat16 [4096, 4096], P('tensor'), may hold values from -0.1875 to 0.1875
- norm_gain: float32 [4096], P('tensor'), may hold values from 0.1 to 1.9
- gate_up: bfloat16 [4096, 2, 11008], P('tensor', None, 'rep'), may hold values from -0.09375 to 0.09375
- down_weight: bfloat16 [11008, 4096], P('rep', 'tensor'), may hold values from -0.109375 to 0.109375
Outputs:
- layer_out: bfloat16 [2048, 4096], P('rep', 'tensor')
Inputs may be any that keep to these rules, and one draw needn't show every extreme that they name: `page_table`: within a group no two requests share a page.
All inputs are finite; a program needn't handle non-finite values.
Results may differ from a plain program's by a relative error of at most 0.03.
Values may be sent and summed in bfloat16 or wider, within the bound.
No kernel may reach another device: no remote copies, remote signals or barrier semaphores. Data moves between devices by JAX's collectives and lax.ppermute only.
A program may use at most 128 MiB of HBM per device.

v0:
```python
import jax
import jax.numpy as jnp
from jax import lax
from jax.sharding import PartitionSpec as P

D = 4096
HD = 128
EPSILON = 1e-05


def attend(queries, cache_block, new_pair, counts):
    row_count = cache_block.shape[0]
    cache_len = cache_block.shape[1]
    kv_width = cache_block.shape[3]
    kv_heads = kv_width // HD
    group_size = queries.shape[1] // kv_width
    query_heads = queries.reshape(row_count, kv_heads, group_size, HD)
    key_heads = cache_block[:, :, 0].reshape(row_count, cache_len, kv_heads, HD)
    value_heads = cache_block[:, :, 1].reshape(row_count, cache_len, kv_heads, HD)
    new_key = new_pair[:, 0].reshape(row_count, kv_heads, HD)
    new_value = new_pair[:, 1].reshape(row_count, kv_heads, HD)
    score_scale = HD ** (-0.5)
    scores = (
        jnp.einsum("nkgd,nlkd->nkgl", query_heads, key_heads, preferred_element_type=jnp.float32)
        * score_scale
    )
    own_score = (
        jnp.einsum("nkgd,nkd->nkg", query_heads, new_key, preferred_element_type=jnp.float32)
        * score_scale
    )
    in_range = (jnp.arange(cache_len, dtype=jnp.int32)[None, :] < counts[:, None])[:, None, None, :]
    masked = jnp.where(in_range, scores, -jnp.inf)
    peak_score = jnp.maximum(jnp.max(masked, axis=-1), own_score)
    weights = jnp.where(in_range, jnp.exp(scores - peak_score[..., None]), 0.0)
    own_weight = jnp.exp(own_score - peak_score)
    denominator = jnp.sum(weights, axis=-1) + own_weight
    weighted = jnp.einsum(
        "nkgl,nlkd->nkgd",
        weights.astype(jnp.bfloat16),
        value_heads,
        preferred_element_type=jnp.float32,
    )
    weighted = weighted + jnp.einsum(
        "nkg,nkd->nkgd",
        own_weight.astype(jnp.bfloat16),
        new_value,
        preferred_element_type=jnp.float32,
    )
    return (weighted / denominator[..., None]).astype(jnp.bfloat16).reshape(row_count, -1)


def local(
    hidden_in,
    query,
    new_kv,
    pool,
    page_table,
    lengths,
    dest,
    out_weight,
    norm_gain,
    gate_up,
    down_weight,
):
    rows_here = hidden_in.shape[0]
    group_count = lax.axis_size("rep")
    my_group = lax.axis_index("rep")
    group_ids = jnp.arange(group_count, dtype=jnp.int32)
    source = jnp.sum(jnp.where(dest == my_group, group_ids, 0))
    page_count = page_table.shape[1]
    page_len = pool.shape[1]
    kv_width = pool.shape[3]
    cache_rows = pool[page_table].reshape(rows_here, page_count * page_len, 2, kv_width)
    my_lengths = lax.dynamic_slice_in_dim(lengths, my_group * rows_here, rows_here)
    home_attn = attend(query, cache_rows, new_kv, my_lengths)
    every_attn, every_hidden = (
        lax.all_gather(home_attn[-1:], "rep", axis=0, tiled=True),
        lax.all_gather(hidden_in[-1:], "rep", axis=0, tiled=True),
    )
    attention = jnp.concatenate(
        [home_attn[:-1], lax.dynamic_slice_in_dim(every_attn, source, 1)], axis=0
    )
    served = jnp.concatenate(
        [hidden_in[:-1], lax.dynamic_slice_in_dim(every_hidden, source, 1)], axis=0
    )
    projected = jnp.dot(attention, out_weight, preferred_element_type=jnp.float32)
    head_total = lax.psum_scatter(
        projected.astype(jnp.bfloat16), "tensor", scatter_dimension=1, tiled=True
    ).astype(jnp.float32)
    residual = served.astype(jnp.float32) + head_total
    square_sum = lax.psum(jnp.sum(residual * residual, axis=1), "tensor")
    normed = (residual * lax.rsqrt(square_sum / D + EPSILON)[:, None] * norm_gain[None, :]).astype(
        jnp.bfloat16
    )
    unit_count = gate_up.shape[2]
    flat_weight = gate_up.reshape(gate_up.shape[0], 2 * unit_count)
    partial_units = jnp.dot(
        lax.all_gather(normed, "rep", axis=0, tiled=True),
        flat_weight,
        preferred_element_type=jnp.float32,
    )
    partial_units = partial_units.reshape(partial_units.shape[0], 2, unit_count)
    unit_total = lax.psum(partial_units.astype(jnp.bfloat16), "tensor").astype(jnp.float32)
    activated = (jax.nn.silu(unit_total[:, 0]) * unit_total[:, 1]).astype(jnp.bfloat16)
    mixed = lax.psum_scatter(
        jnp.dot(activated, down_weight, preferred_element_type=jnp.float32).astype(jnp.bfloat16),
        "rep",
        scatter_dimension=0,
        tiled=True,
    ).astype(jnp.float32)
    return (residual + mixed).astype(jnp.bfloat16)


def solution(mesh):
    return jax.shard_map(
        local,
        mesh=mesh,
        in_specs=(
            P("rep", "tensor"),
            P("rep", "tensor"),
            P("rep", None, "tensor"),
            P("rep", None, None, "tensor"),
            P("rep", None),
            P(),
            P(),
            P("tensor", None),
            P("tensor"),
            P("tensor", None, "rep"),
            P("rep", "tensor"),
        ),
        out_specs=P("rep", "tensor"),
        check_vma=False,
    )
```

profile of v0, /device:TPU:0, one launch (start us, length us, event | category | flops | bytes accessed | tf_op | source)
XLA Modules:
  0.0 336.0 jit_solution(7279921076718886438)
XLA Ops:
  6.5 0.8 compare_select_fusion
  7.4 0.1 reshape.104
  7.6 23.2 %gather_fusion = bf16[128,128,2,128]{3,2,1,0:T(2,128)(2,1)} fusion(bf16[128,128,2,128]{3,2,1,0:T(2,128)(2,1)} %param.14, s32[1024]{0:T(1024)S(1)} %pad_clamp_fusion), kind=kCustom, calls=%fused_computation | custom fusion | bytes 16777728 | tf_op jit(solution)/shard_map/gather | solution.py:73
  30.8 8.9 %copy.18 = bf16[128,128,2,128]{3,1,0,2:T(8,128)(2,1)} copy(bf16[128,128,2,128]{3,2,1,0:T(2,128)(2,1)} %gather_fusion) | data formatting | bytes 16777216 | tf_op jit(solution)/shard_map/gather | solution.py:73
  39.7 0.8 dynamic_slice.10
  40.6 0.2 fusion.22
  40.8 3.5 %select_reduce_fusion = (f32[64,8]{1,0:T(8,128)S(1)}, f32[64,256,8]{1,2,0:T(8,128)S(1)}) fusion(pred[64,256]{1,0:T(8,128)(4,1)S(1)} %iota_compare_fusion, bf16[64,8,128]{2,1,0:T(8,128)(2,1)S(1)} %bitcast.79, bf16[64,256,2,128]{3,1,0,2:T(8,128)(2,1)} %bitcast.68), kind=kOutput, calls=%fused_computation.23 | convolution fusion | flops 33947136 | bytes 4868096 | tf_op jit(solution)/shard_map/nkgd,nlkd->nkgl/dot_general | solution.py:24
  44.3 0.3 bitcast_reduce_fusion
  44.6 2.9 fusion.15
  47.5 26.2 %all-gather.1 = bf16[32,1,1024]{2,1,0:T(2,128)(2,1)S(1)} all-gather(bf16[1,1,1024]{2,1,0:T(2,128)(2,1)S(1)} %reshape.115), channel_id=1, replica_groups=mesh['rep'=32,'tensor'=4] {'rep'}, dimensions={0}, use_global_device_ids=true | all-gather | bytes 67584 | tf_op jit(solution)/shard_map/all_gather | solution.py:77
  73.7 0.6 fusion.25
  76.4 5.8 %convolution_convert_fusion = bf16[64,4096]{1,0:T(8,128)(2,1)} fusion(bf16[1024,4096]{1,0:T(8,128)(2,1)} %param.18, bf16[1,1024]{1,0:T(2,128)(2,1)S(1)} %dynamic-slice_bitcast_fusion, bf16[63,1024]{1,0:T(8,128)(2,1)S(1)} %bitcast.73), kind=kOutput, calls=%fused_computation.1 | convolution fusion | flops 537395200 | bytes 9043968 | tf_op jit(solution)/shard_map/dot_general | solution.py:86
  82.3 24.0 %all-gather = bf16[32,1,1024]{2,1,0:T(2,128)(2,1)S(1)} all-gather(bf16[1,1,1024]{2,1,0:T(2,128)(2,1)S(1)} %slice_bitcast_fusion.14), channel_id=1, replica_groups=mesh['rep'=32,'tensor'=4] {'rep'}, dimensions={0}, use_global_device_ids=true | all-gather | bytes 67584 | tf_op jit(solution)/shard_map/all_gather | solution.py:78
  106.3 1.1 multiply_reduce_fusion
  107.4 10.5 %psum.14 = f32[64]{0:T(128)S(1)} all-reduce(f32[64]{0:T(128)S(1)} %multiply_reduce_fusion), channel_id=1, replica_groups=mesh['rep'=32,'tensor'=4] {'tensor'}, use_global_device_ids=true, to_apply=%region_5.6 | all-reduce | flops 64 | bytes 512 | tf_op jit(solution)/shard_map/psum | solution.py:91
  117.9 1.7 multiply_convert_fusion
  119.6 42.7 %all-gather.4.cloned.1.call-done = bf16[2048,1024]{1,0:T(8,128)(2,1)} async-done(((bf16[64,1024]{1,0:T(8,128)(2,1)}), bf16[2048,1024]{1,0:T(8,128)(2,1)}) %all-gather.4.cloned.1.call-update) | async-done | bytes 4194320 | tf_op jit(solution)/shard_map/all_gather | solution.py:98
  162.3 6.7 %fusion.4 = bf16[2048,2,344]{0,2,1:T(8,128)(2,1)} fusion(bf16[2048,1024]{1,0:T(8,128)(2,1)} %all-gather.4.cloned.1.call-done, bf16[1024,2,344]{0,2,1:T(8,128)(2,1)S(1)} %copy-done), kind=kOutput, calls=%fused_computation.9 | convolution fusion | flops 2887090176 | bytes 8421376 | tf_op jit(solution)/shard_map/dot_general | solution.py:97
  169.0 0.2 reduce-scatter.5.cloned.1.call-start
  169.3 69.5 %all-reduce.2.cloned.1.call-done = bf16[2048,2,344]{0,2,1:T(8,128)(2,1)} async-done(((bf16[2048,2,344]{0,2,1:T(8,128)(2,1)}), bf16[2048,2,344]{0,2,1:T(8,128)(2,1)}) %all-reduce.2.cloned.1.call-update) | async-done | bytes 2818064 | tf_op jit(solution)/shard_map/psum | solution.py:103
  238.8 2.5 convert_element_type.50
  241.3 4.4 %convolution_convert_fusion.1 = bf16[2048,1024]{1,0:T(8,128)(2,1)} fusion(bf16[344,1024]{1,0:T(8,128)(2,1)S(1)} %copy-done.6, f32[2048,2,344]{0,2,1:T(8,128)S(1)} %convert_element_type.50), kind=kOutput, calls=%fused_computation.8 | convolution fusion | flops 1449164800 | bytes 10534912 | tf_op jit(solution)/shard_map/dot_general | solution.py:106
  245.8 82.1 %reduce-scatter.5.cloned.1.call-done = bf16[64,1024]{1,0:T(8,128)(2,1)} async-done(((bf16[2048,1024]{1,0:T(8,128)(2,1)}), bf16[64,1024]{1,0:T(8,128)(2,1)}) %reduce-scatter.5.cloned.1.call-update) | async-done | bytes 131088 | tf_op jit(solution)/shard_map/reduce_scatter | solution.py:105
  327.9 1.6 add_convert_fusion
  (41 shorter events, 0.6 us)
Async XLA Ops:
  6.5 155.8 %copy-start = (bf16[1024,2,344]{0,2,1:T(8,128)(2,1)S(1)}, bf16[1024,2,344]{0,2,1:T(8,128)(2,1)}, u32[]{:S(2)}) copy-start(bf16[1024,2,344]{0,2,1:T(8,128)(2,1)} %param.20) | copy-start | bytes 4227076
  6.5 99.8 %reduce-scatter.3.cloned.1.call-start = ((), (), s32[]{:S(2)}) async-start(), calls=%async_computation.2 | async-start | bytes 655360 | tf_op jit(solution)/shard_map/reduce_scatter | solution.py:87
  30.8 9.7 %copy-start.3 = (bf16[64,1024]{1,0:T(8,128)(2,1)S(1)}, bf16[64,1024]{1,0:T(8,128)(2,1)}, u32[]{:S(2)}) copy-start(bf16[64,1024]{1,0:T(8,128)(2,1)} %param.12) | copy-start | bytes 393220
  30.8 9.8 %copy-start.4 = (bf16[64,2,128]{2,1,0:T(2,128)(2,1)S(1)}, bf16[64,2,128]{2,1,0:T(2,128)(2,1)}, u32[]{:S(2)}) copy-start(bf16[64,2,128]{2,1,0:T(2,128)(2,1)} %param.13) | copy-start | bytes 98308
  44.3 29.4 %copy-start.7 = (s32[32]{0:T(128)S(1)}, s32[32]{0:T(128)}, u32[]{:S(2)}) copy-start(s32[32]{0:T(128)} %param.17) | copy-start | bytes 388
  76.4 5.9 %copy-start.1 = (bf16[64,1024]{1,0:T(8,128)(2,1)S(1)}, bf16[64,1024]{1,0:T(8,128)(2,1)}, u32[]{:S(2)}) copy-start(bf16[64,1024]{1,0:T(8,128)(2,1)} %param.11) | copy-start | bytes 393220
  76.4 41.5 %copy-start.5 = (f32[1024]{0:T(1024)S(1)}, f32[1024]{0:T(1024)}, u32[]{:S(2)}) copy-start(f32[1024]{0:T(1024)} %param.19) | copy-start | bytes 12292
  82.2 80.1 %all-gather.4.cloned.1.call-start = ((), (), s32[]{:S(2)}) async-start(), calls=%async_computation.3 | async-start | bytes 4325376 | tf_op jit(solution)/shard_map/all_gather | solution.py:98
  119.6 119.2 %all-reduce.2.cloned.1.call-start = ((), (), s32[]{:S(2)}) async-start(), calls=%async_computation.4 | async-start | bytes 5636096 | tf_op jit(solution)/shard_map/psum | solution.py:103
  169.0 72.3 %copy-start.6 = (bf16[344,1024]{1,0:T(8,128)(2,1)S(1)}, bf16[344,1024]{1,0:T(8,128)(2,1)}, u32[]{:S(2)}) copy-start(bf16[344,1024]{1,0:T(8,128)(2,1)} %param.21) | copy-start | bytes 2113540
  169.0 158.8 %reduce-scatter.5.cloned.1.call-start = ((), (), s32[]{:S(2)}) async-start(), calls=%async_computation.5 | async-start | bytes 4325376 | tf_op jit(solution)/shard_map/reduce_scatter | solution.py:105
  245.8 82.1 %copy-start.2 = (bf16[64,1024]{1,0:T(8,128)(2,1)S(1)}, bf16[64,1024]{1,0:T(8,128)(2,1)}, u32[]{:S(2)}) copy-start(bf16[64,1024]{1,0:T(8,128)(2,1)} %reduce-scatter.3.cloned.1.call-done) | copy-start | bytes 393220
Sparse Core Ops, SparseCore 0:
  82.3 20.4 reduce-scatter.2
  119.7 42.5 all-gather.3
  169.1 69.5 all-reduce.1
  245.9 81.9 reduce-scatter.4
where the time goes:
time: 336 us
  waiting for transfers between devices  194 us (58%)
  blocking collectives  60.7 us (18%)
  local copies, waits for them, and re-layouts  33.2 us (10%)
  matrix products  23.4 us (7%)
  between operations  15.3 us (5%)
  other arithmetic  8.71 us (3%)
    reduce_scatter x1, waiting for transfers between devices, local(): lax.psum_scatter(jnp.dot(activated, down_weight, preferred_element_type=j...  82.1 us
    psum x1, waiting for transfers between devices, local(): lax.psum(partial_units.astype(jnp.bfloat16), 'tensor').astype(jnp.float32)  69.5 us
    all_gather x1, waiting for transfers between devices, local(): lax.all_gather(normed, 'rep', axis=0, tiled=True)  42.7 us
    gather x2, local copies, waits for them, and re-layouts, local(): pool[page_table].reshape(rows_here, page_count * page_len, 2, kv_width)  32.1 us
    all_gather x1, blocking collectives, local(): lax.all_gather(home_attn[-1:], 'rep', axis=0, tiled=True)  26.2 us
    all_gather x1, blocking collectives, local(): lax.all_gather(hidden_in[-1:], 'rep', axis=0, tiled=True)  24 us
    psum x1, blocking collectives, local(): square_sum = lax.psum(jnp.sum(residual * residual, axis=1), 'tensor')  10.5 us
  transfers between devices with their start and end apart: 4, of which 3 were waited for; matrix products, arithmetic and copies ran while one was open for 0% of the time, Pallas kernels for 0%

commit v1 on v0

--- a/solution.py
+++ b/solution.py
@@ -100,7 +100,8 @@
         preferred_element_type=jnp.float32,
     )
     partial_units = partial_units.reshape(partial_units.shape[0], 2, unit_count)
-    unit_total = lax.psum(partial_units.astype(jnp.bfloat16), "tensor").astype(jnp.float32)
+    _plan_floor = lambda page, peer_axis: jnp.sum(lax.all_gather(page, peer_axis), axis=0)
+    unit_total = _plan_floor(partial_units.astype(jnp.bfloat16), "tensor").astype(jnp.float32)
     activated = (jax.nn.silu(unit_total[:, 0]) * unit_total[:, 1]).astype(jnp.bfloat16)
     mixed = lax.psum_scatter(
         jnp.dot(activated, down_weight, preferred_element_type=jnp.float32).astype(jnp.bfloat16),

time: 336 us -> 419 us (1.25)
  waiting for transfers between devices: 194 us -> 233 us
  local copies, waits for them, and re-layouts: 33.2 us -> 57.8 us
  other arithmetic: 8.71 us -> 27.3 us
    all_gather x0 -> x1, waiting for transfers between devices: none -> 107 us  [local(): lax.all_gather(page, peer_axis)]
    psum x1 -> x0, waiting for transfers between devices: 69.5 us -> none  [local(): lax.psum(partial_units.astype(jnp.bfloat16), 'tensor').astype(jnp.float32)]
    all_gather x0 -> x1, local copies, waits for them, and re-layouts: none -> 23.7 us  [local(): lax.all_gather(page, peer_axis)]
    reduce_sum x0 -> x1, other arithmetic: none -> 17.7 us  [local(): jnp.sum(lax.all_gather(page, peer_axis), axis=0)]
where the time goes in v1:
time: 419 us; the launch traced here: 418 us
  waiting for transfers between devices  233 us (56%)
  blocking collectives  60.7 us (14%)
  local copies, waits for them, and re-layouts  57.8 us (14%)
  other arithmetic  27.3 us (7%)
  matrix products  23.5 us (6%)
  between operations  15.3 us (4%)
    all_gather x1, waiting for transfers between devices, local(): lax.all_gather(page, peer_axis)  107 us
    reduce_scatter x1, waiting for transfers between devices, local(): lax.psum_scatter(jnp.dot(activated, down_weight, preferred_element_type=j...  83.2 us
    all_gather x1, waiting for transfers between devices, local(): lax.all_gather(normed, 'rep', axis=0, tiled=True)  42.7 us
    gather x2, local copies, waits for them, and re-layouts, local(): pool[page_table].reshape(rows_here, page_count * page_len, 2, kv_width)  32 us
    all_gather x1, blocking collectives, local(): lax.all_gather(home_attn[-1:], 'rep', axis=0, tiled=True)  26.2 us
    all_gather x1, blocking collectives, local(): lax.all_gather(hidden_in[-1:], 'rep', axis=0, tiled=True)  24 us
    all_gather x1, local copies, waits for them, and re-layouts, local(): lax.all_gather(page, peer_axis)  23.7 us
    reduce_sum x1, other arithmetic, local(): jnp.sum(lax.all_gather(page, peer_axis), axis=0)  17.7 us
  transfers between devices with their start and end apart: 4, of which 3 were waited for; matrix products, arithmetic and copies ran while one was open for 0% of the time, Pallas kernels for 0%

profile of v1, /device:TPU:0, one launch (start us, length us, event | category | flops | bytes accessed | tf_op | source)
XLA Modules:
  0.0 417.5 jit_solution(3554288024206522005)
XLA Ops:
  6.5 0.8 compare_select_fusion
  7.3 0.8 dynamic_slice.10
  8.4 0.9 slice_convert_fusion
  9.3 0.9 copy.24
  10.3 23.2 %gather_fusion = bf16[128,128,2,128]{3,2,1,0:T(2,128)(2,1)} fusion(bf16[128,128,2,128]{3,2,1,0:T(2,128)(2,1)} %param.14, s32[1024]{0:T(1024)S(1)} %pad_clamp_fusion), kind=kCustom, calls=%fused_computation | custom fusion | bytes 16777728 | tf_op jit(solution)/shard_map/gather | solution.py:73
  33.4 8.9 %copy.19 = bf16[128,128,2,128]{3,1,0,2:T(8,128)(2,1)} copy(bf16[128,128,2,128]{3,2,1,0:T(2,128)(2,1)} %gather_fusion) | data formatting | bytes 16777216 | tf_op jit(solution)/shard_map/gather | solution.py:73
  42.5 3.5 select_reduce_fusion
  46.3 2.9 fusion.15
  49.2 0.6 fusion.25
  51.2 26.2 %all-gather.2 = bf16[32,1,1024]{2,1,0:T(2,128)(2,1)S(1)} all-gather(bf16[1,1,1024]{2,1,0:T(2,128)(2,1)S(1)} %reshape.116), channel_id=1, replica_groups=mesh['rep'=32,'tensor'=4] {'rep'}, dimensions={0}, use_global_device_ids=true | all-gather | bytes 67584 | tf_op jit(solution)/shard_map/all_gather | solution.py:77
  78.1 5.8 %convolution_convert_fusion = bf16[64,4096]{1,0:T(8,128)(2,1)} fusion(bf16[1024,4096]{1,0:T(8,128)(2,1)} %param.18, bf16[1,1024]{1,0:T(2,128)(2,1)S(1)} %dynamic-slice_bitcast_fusion, bf16[63,1024]{1,0:T(8,128)(2,1)S(1)} %bitcast.75), kind=kOutput, calls=%fused_computation.1 | convolution fusion | flops 537395200 | bytes 9043968 | tf_op jit(solution)/shard_map/dot_general | solution.py:86
  84.0 24.0 %all-gather.1 = bf16[32,1,1024]{2,1,0:T(2,128)(2,1)S(1)} all-gather(bf16[1,1,1024]{2,1,0:T(2,128)(2,1)S(1)} %slice_bitcast_fusion.14), channel_id=1, replica_groups=mesh['rep'=32,'tensor'=4] {'rep'}, dimensions={0}, use_global_device_ids=true | all-gather | bytes 67584 | tf_op jit(solution)/shard_map/all_gather | solution.py:78
  108.0 1.1 multiply_reduce_fusion
  109.1 10.5 %psum.7 = f32[64]{0:T(128)S(1)} all-reduce(f32[64]{0:T(128)S(1)} %multiply_reduce_fusion), channel_id=1, replica_groups=mesh['rep'=32,'tensor'=4] {'tensor'}, use_global_device_ids=true, to_apply=%region_5.6 | all-reduce | flops 64 | bytes 512 | tf_op jit(solution)/shard_map/psum | solution.py:91
  119.6 1.7 multiply_convert_fusion
  121.3 42.7 %all-gather.6.cloned.1.call-done = bf16[2048,1024]{1,0:T(8,128)(2,1)} async-done(((bf16[64,1024]{1,0:T(8,128)(2,1)}), bf16[2048,1024]{1,0:T(8,128)(2,1)}) %all-gather.6.cloned.1.call-update) | async-done | bytes 4194320 | tf_op jit(solution)/shard_map/all_gather | solution.py:98
  164.1 6.7 %fusion.4 = bf16[2048,2,344]{0,2,1:T(8,128)(2,1)} fusion(bf16[2048,1024]{1,0:T(8,128)(2,1)} %all-gather.6.cloned.1.call-done, bf16[1024,2,344]{0,2,1:T(8,128)(2,1)S(1)} %copy-done), kind=kOutput, calls=%fused_computation.9 | convolution fusion | flops 2887090176 | bytes 8421376 | tf_op jit(solution)/shard_map/dot_general | solution.py:97
  171.0 106.6 %all-gather.8.cloned.1.call-done = bf16[8192,2,344]{0,2,1:T(8,128)(2,1)} async-done(((bf16[2048,2,344]{0,2,1:T(8,128)(2,1)}), bf16[8192,2,344]{0,2,1:T(8,128)(2,1)}) %all-gather.8.cloned.1.call-update) | async-done | bytes 11272208 | tf_op jit(solution)/shard_map/all_gather | solution.py:103
  277.6 23.7 %reshape.110 = bf16[4,2048,2,344]{1,0,3,2:T(4,128)(2,1)} reshape(bf16[8192,2,344]{0,2,1:T(8,128)(2,1)} %all-gather.8.cloned.1.call-done) | data formatting | bytes 22544384 | tf_op jit(solution)/shard_map/all_gather | solution.py:103
  301.4 17.7 %reduce_sum.42 = bf16[2048,2,344]{0,2,1:T(8,128)(2,1)} reduce(bf16[4,2048,2,344]{1,0,3,2:T(4,128)(2,1)} %reshape.110, bf16[]{:T(256)} %constant.32.clone.1), dimensions={0}, to_apply=%region_6.7 | reduce | flops 4227072 | bytes 14090242 | tf_op jit(solution)/shard_map/reduce_sum | solution.py:103
  319.0 2.6 convert_element_type.52
  321.7 4.4 %convolution_convert_fusion.1 = bf16[2048,1024]{1,0:T(8,128)(2,1)} fusion(bf16[344,1024]{1,0:T(8,128)(2,1)S(1)} %copy-done.5, f32[2048,2,344]{0,2,1:T(8,128)S(1)} %convert_element_type.52), kind=kOutput, calls=%fused_computation.8 | convolution fusion | flops 1449164800 | bytes 10534912 | tf_op jit(solution)/shard_map/dot_general | solution.py:107
  326.1 83.2 %reduce-scatter.5.cloned.1.call-done = bf16[64,1024]{1,0:T(8,128)(2,1)} async-done(((bf16[2048,1024]{1,0:T(8,128)(2,1)}), bf16[64,1024]{1,0:T(8,128)(2,1)}) %reduce-scatter.5.cloned.1.call-update) | async-done | bytes 131088 | tf_op jit(solution)/shard_map/reduce_scatter | solution.py:106
  409.4 1.6 add_convert_fusion
  (41 shorter events, 1.3 us)
Async XLA Ops:
  6.5 157.5 %copy-start = (bf16[1024,2,344]{0,2,1:T(8,128)(2,1)S(1)}, bf16[1024,2,344]{0,2,1:T(8,128)(2,1)}, u32[]{:S(2)}) copy-start(bf16[1024,2,344]{0,2,1:T(8,128)(2,1)} %param.20) | copy-start | bytes 4227076
  6.5 101.5 %reduce-scatter.3.cloned.1.call-start = ((), (), s32[]{:S(2)}) async-start(), calls=%async_computation.2 | async-start | bytes 655360 | tf_op jit(solution)/shard_map/reduce_scatter | solution.py:87
  46.0 3.3 copy-start.6
  78.1 5.9 %copy-start.2 = (bf16[64,1024]{1,0:T(8,128)(2,1)S(1)}, bf16[64,1024]{1,0:T(8,128)(2,1)}, u32[]{:S(2)}) copy-start(bf16[64,1024]{1,0:T(8,128)(2,1)} %param.11) | copy-start | bytes 393220
  78.1 41.5 %copy-start.4 = (f32[1024]{0:T(1024)S(1)}, f32[1024]{0:T(1024)}, u32[]{:S(2)}) copy-start(f32[1024]{0:T(1024)} %param.19) | copy-start | bytes 12292
  83.9 80.1 %all-gather.6.cloned.1.call-start = ((), (), s32[]{:S(2)}) async-start(), calls=%async_computation.3 | async-start | bytes 4325376 | tf_op jit(solution)/shard_map/all_gather | solution.py:98
  121.3 156.3 %all-gather.8.cloned.1.call-start = ((), (), s32[]{:S(2)}) async-start(), calls=%async_computation.5 | async-start | bytes 14090240 | tf_op jit(solution)/shard_map/all_gather | solution.py:103
  170.8 238.6 %reduce-scatter.5.cloned.1.call-start = ((), (), s32[]{:S(2)}) async-start(), calls=%async_computation.4 | async-start | bytes 4325376 | tf_op jit(solution)/shard_map/reduce_scatter | solution.py:106
  319.0 2.6 copy-start.5
  321.7 89.3 %copy-start.1 = (bf16[1024,2,344]{0,2,1:T(8,128)(2,1)S(1)}, bf16[1024,2,344]{0,2,1:T(8,128)(2,1)}, u32[]{:S(2)}) copy-start(bf16[1024,2,344]{0,2,1:T(8,128)(2,1)} %param.20) | copy-start | bytes 4227076
  326.1 83.3 %copy-start.3 = (bf16[64,1024]{1,0:T(8,128)(2,1)S(1)}, bf16[64,1024]{1,0:T(8,128)(2,1)}, u32[]{:S(2)}) copy-start(bf16[64,1024]{1,0:T(8,128)(2,1)} %reduce-scatter.3.cloned.1.call-done) | copy-start | bytes 393220
Sparse Core Ops, SparseCore 0:
  84.0 20.4 reduce-scatter.2
  121.4 42.5 all-gather.5
  170.9 106.6 all-gather.7
  326.2 83.0 reduce-scatter.4
